TPU v7x, 32 devices: a whole 2x2x4 slice. The times are simulated.
32 devices in a mesh: grp: 2 (over y), dep: 4 (over z), hgt: 2 (over x), wid: 2 (over core).
Axes of the slice: x: 2, y: 2, z: 4, core: 2. Of those that a mesh axis runs over, the one named last changes fastest.
Arguments:
- features: bfloat16 [64, 8, 16, 256], P('grp', 'wid', 'dep', 'hgt'), parts along dimension 0, may hold values from -6 to 6
- cotangent: bfloat16 [64, 8, 16, 256], P('grp', 'wid', 'dep', 'hgt'), parts along dimension 0, may hold values from -6 to 6
- w_stem: bfloat16 [3, 3, 3, 32, 32], replicated, may hold values from -0.21875 to 0.21875
- w_middle: bfloat16 [3, 3, 3, 32, 64], replicated, may hold values from -0.21875 to 0.21875
- w_bottom: bfloat16 [3, 3, 3, 64, 128], replicated, may hold values from -0.15625 to 0.15625
- w_rise: bfloat16 [3, 3, 3, 192, 64], replicated, may hold values from -0.078125 to 0.078125
- w_final: bfloat16 [3, 3, 3, 96, 32], replicated, may hold values from -0.125 to 0.125
Outputs:
- output: bfloat16 [64, 8, 16, 256], P('grp', 'wid', 'dep', 'hgt'), parts along dimension 0
- grad_stem: float32 [6, 3, 3, 32, 32], P('grp'), parts along dimension 0
- grad_middle: float32 [6, 3, 3, 32, 64], P('grp'), parts along dimension 0
- grad_bottom: float32 [6, 3, 3, 64, 128], P('grp'), parts along dimension 0
- grad_rise: float32 [6, 3, 3, 192, 64], P('grp'), parts along dimension 0
- grad_final: float32 [6, 3, 3, 96, 32], P('grp'), parts along dimension 0
- half_grad: float32 [64, 4, 8, 128], P('grp', 'wid', 'dep', 'hgt'), parts along dimension 0
There are 2 independent parts, one for each index of `grp`. A program takes and returns all parts, laid end to end along the dimension named above; an argument that names none is the same for every part. Nothing has to cross between parts.
All inputs are finite; a program needn't handle non-finite values.
Results may differ from a plain program's by a relative error of at most 0.012.
Values may be sent and summed in bfloat16 or wider, within the bound.
A program may use at most 128 MiB of HBM per device.

v0:
```python
import functools
import math

import jax
import jax.numpy as jnp
from jax import lax
from jax.experimental import pallas as pl
from jax.experimental.pallas import tpu as pltpu
from jax.sharding import PartitionSpec as P

BF, F32 = jnp.bfloat16, jnp.float32
AXES = ("grp", "dep", "hgt", "wid")


def mm(a, b):
    return lax.dot_general(a, b, (((1,), (0,)), ((), ())), preferred_element_type=F32)


def mm_nt(a, b):
    return lax.dot_general(a, b, (((1,), (1,)), ((), ())), preferred_element_type=F32)


def mm_split(a, b):
    high = a.astype(BF)
    low = (a - high.astype(F32)).astype(BF)
    return mm(high, b) + mm(low, b)


def silu(v):
    return v * jax.nn.sigmoid(v)


def slope(v):
    g = jax.nn.sigmoid(v)
    return g * (1.0 + v * (1.0 - g))


def pattern(lanes, test):
    row = lax.broadcasted_iota(jnp.int32, (lanes, lanes), 0)
    col = lax.broadcasted_iota(jnp.int32, (lanes, lanes), 1)
    return jnp.where(test(row, col), 1.0, 0.0)


class Halo:
    def __init__(self, index, rows, edges, own, span, sems):
        self.index, self.rows, self.edges, self.own = index, rows, edges, own
        self.w, self.d, self.h = span
        self.send, self.recv = sems

    def fill_edges(self):
        lanes = self.own.shape[1]
        lane = lax.broadcasted_iota(jnp.int32, self.own.shape, 1)
        tile = jnp.zeros(self.own.shape, F32)
        for a in range(self.w):
            for b in range(self.d):
                r = a * self.d + b
                row = self.rows[a + 1, b + 1].astype(F32)
                tile = jnp.where(lane == r, row[:, 0:1], tile)
                tile = jnp.where(lane == lanes // 2 + r, row[:, self.h - 1 : self.h], tile)
        self.own[...] = tile.astype(BF)

    def copies(self, build=True):
        place = {name: lax.axis_index(name) for name in AXES}
        size = {name: lax.axis_size(name) for name in AXES}

        def choices(name):
            i, n = place[name], size[name]
            if n == 1:
                return [(0, 0, True, True)]
            if n == 2:
                return [(0, 0, True, True), (1, 1 - 2 * i, True, True)]
            return [(0, 0, True, True), (1, 1, i < n - 1, i > 0), (2, -1, i > 0, i < n - 1)]

        def cells(step, code, count):
            if code == 0:
                return pl.ds(1, count), pl.ds(1, count)
            up = (1 + step) // 2
            return pl.ds(1 + (count - 1) * up, 1), pl.ds((count + 1) * (1 - up), 1)

        out = []
        for cw, sw, ow, iw in choices("wid"):
            for cd, sd, od, id_ in choices("dep"):
                for ch, sh, oh, ih in choices("hgt"):
                    if cw == 0 and cd == 0 and ch == 0:
                        continue
                    slot = self.index * 27 + (cw * 3 + cd) * 3 + ch
                    target = {"wid": place["wid"] + sw, "dep": place["dep"] + sd, "hgt": place["hgt"] + sh}
                    if not build:
                        out.append((target, [c for c in (ow, od, oh) if c is not True], [c for c in (iw, id_, ih) if c is not True]))
                        continue
                    if ch == 0:
                        from_w, to_w = cells(sw, cw, self.w)
                        from_d, to_d = cells(sd, cd, self.d)
                        source = self.rows.at[from_w, from_d]
                        dest = self.rows.at[to_w, to_d]
                    else:
                        source = self.own
                        dest = self.edges.at[(1 - sh) // 2, 1 - sw, 1 - sd]
                    copy = pltpu.make_async_remote_copy(
                        src_ref=source,
                        dst_ref=dest,
                        send_sem=self.send.at[slot],
                        recv_sem=self.recv.at[slot],
                        device_id=target,
                        device_id_type=pl.DeviceIdType.MESH,
                    )
                    out.append((copy, [c for c in (ow, od, oh) if c is not True], [c for c in (iw, id_, ih) if c is not True]))
        return out

    @staticmethod
    def guarded(conditions, action):
        if not conditions:
            action()
        else:
            pl.when(functools.reduce(jnp.logical_and, conditions))(action)

    def start(self):
        self.fill_edges()
        for copy, can_send, _ in self.copies():
            self.guarded(can_send, copy.start)

    def wait(self):
        for copy, _, can_take in self.copies():
            self.guarded(can_take, copy.wait_recv)

    def finish(self):
        for copy, can_send, _ in self.copies():
            self.guarded(can_send, copy.wait_send)

    def shifted(self, a, b, spread=None, fine=None):
        lanes = self.own.shape[1]
        h = self.h if spread is None else 2 * self.h
        row = self.rows[a, b]
        if spread is not None:
            row = mm(row, spread).astype(BF)
        dw = 0 if a == 0 else 2 if a == self.w + 1 else 1
        dd = 0 if b == 0 else 2 if b == self.d + 1 else 1
        r = (self.w - 1, a - 1, 0)[dw] * self.d + (self.d - 1, b - 1, 0)[dd]
        left = self.edges[0, dw, dd].astype(F32)[:, lanes // 2 + r : lanes // 2 + r + 1]
        right = self.edges[1, dw, dd].astype(F32)[:, r : r + 1]
        lane = lax.broadcasted_iota(jnp.int32, row.shape, 1)
        wide = row.astype(F32)
        before = jnp.where(lane == 0, left, pltpu.roll(wide, 1, 1))
        after = jnp.where(lane == h - 1, right, pltpu.roll(wide, lanes - 1, 1))
        if h < lanes:
            before = jnp.where(lane < h, before, 0.0)
            after = jnp.where(lane < h, after, 0.0)
        return before.astype(BF), row, after.astype(BF)


def step_kernel(cfg, *refs):
    (f0, f1, f2, w, d, h) = cfg
    (feat, cot, w_stem, w_mid, w_bot, w_rise, w_fin, b_mid, b_bot, b_rise, b_fin) = refs[:11]
    (output, grads, half_out) = refs[11:14]
    names = ("feat", "cot", "stem", "half", "mid", "quarter", "deep", "ra", "rg", "dg", "mg")
    refs = refs[14:]
    spans = {0: (w, d, h), 1: (w // 2, d // 2, h // 2), 2: (w // 4, d // 4, h // 4)}
    levels = dict(feat=0, cot=0, stem=0, half=1, mid=1, quarter=2, deep=2, ra=1, rg=1, dg=2, mg=1)
    send, recv = refs[0], refs[1]
    halo = {}
    for i, name in enumerate(names):
        rows, edges, own = refs[2 + 3 * i : 5 + 3 * i]
        halo[name] = Halo(i, rows, edges, own, spans[levels[name]], (send, recv))
    rest = refs[2 + 3 * len(names) :]
    (s_feat, s_cot, s_half, s_quarter, s_rise, s_fin, s_rg, s_dg, s_mg) = rest[:9]
    (stem_pre, mid_pre, deep_pre, rise_pre, fb_pool, fb_skip, rb_skip, stem_grad) = rest[9:]

    for item in halo.values():
        item.rows[...] = jnp.zeros(item.rows.shape, BF)
        item.edges[...] = jnp.zeros(item.edges.shape, BF)
    for a in range(w):
        for b in range(d):
            halo["feat"].rows[a + 1, b + 1] = feat[a, b]
            halo["cot"].rows[a + 1, b + 1] = cot[a, b]

    barrier = pltpu.get_barrier_semaphore()
    for target, can_send, _ in halo["feat"].copies(False):
        Halo.guarded(
            can_send,
            functools.partial(
                pl.semaphore_signal, barrier, 1, device_id=target, device_id_type=pl.DeviceIdType.MESH
            ),
        )
    peers = 1
    for name in ("wid", "dep", "hgt"):
        i, n = lax.axis_index(name), lax.axis_size(name)
        peers = peers * (1 + jnp.minimum(i, 1) + jnp.minimum(n - 1 - i, 1))
    pl.semaphore_wait(barrier, peers - 1)

    lanes = h
    pool = pattern(lanes, lambda r, c: r // 2 == c)
    pool_mean = (pool / 8.0).astype(BF)
    pool_sum = pool.astype(BF)
    spread = pattern(lanes, lambda r, c: c // 2 == r)
    spread_mean = (spread / 8.0).astype(BF)
    spread = spread.astype(BF)

    def stack_shifts(name, target):
        item = halo[name]
        for a in range(item.w + 2):
            for b in range(item.d + 2):
                target[a, b] = jnp.concatenate(item.shifted(a, b), axis=0)

    def stack_pair(coarse, fine, target):
        up, low = halo[coarse], halo[fine]
        for a in range(low.w + 2):
            for b in range(low.d + 2):
                one = up.shifted((a + 1) // 2, (b + 1) // 2, spread)
                two = low.shifted(a, b)
                target[a, b] = jnp.concatenate([v for pair in zip(one, two) for v in pair], axis=0)

    def patch(source, a, b, pair):
        parts = []
        for q in range(pair):
            parts.append(
                jnp.concatenate([source[a + ka, b + kb + q] for ka in range(3) for kb in range(3)], axis=0)
            )
        return parts[0] if pair == 1 else jnp.concatenate(parts, axis=1)

    def over_rows(span, body):
        pair = 2 if span[1] % 2 == 0 else 1
        across = span[1] // pair

        def trip(i, _):
            body(i // across, (i % across) * pair, pair)
            return 0

        count = span[0] * across
        if count == 1:
            body(0, 0, pair)
        else:
            lax.fori_loop(0, count, trip, 0)

    def conv(source, weight, span, store):
        def body(a, b, pair):
            result = mm(weight[...], patch(source, a, b, pair))
            for q in range(pair):
                store(a, b + q, result[:, q * lanes : (q + 1) * lanes])

        over_rows(span, body)

    def wgrad_into(base, patches, grad, width):
        groups = lanes // width
        count = patches.shape[0] // groups
        for g in range(groups):
            pieces = [jnp.zeros_like(grad)] * groups
            pieces[g] = grad
            full = pieces[0] if groups == 1 else jnp.concatenate(pieces, axis=0)
            part = mm_nt(patches[g * count : (g + 1) * count], full)
            grads[base : base + count] += part

    def grad_row(ref, a, b, pair, pad):
        parts = [ref[a + pad, b + pad + q] for q in range(pair)]
        return parts[0] if pair == 1 else jnp.concatenate(parts, axis=1)

    sizes = [27 * f0 * f0, 27 * f0 * f1, 27 * f1 * f2, 27 * (f2 + f1) * f1, 27 * (f1 + f0) * f0]
    bases = [sum(sizes[:i]) // lanes for i in range(5)]
    grads[...] = jnp.zeros(grads.shape, F32)

    halo["feat"].start()
    halo["cot"].start()
    halo["feat"].wait()
    stack_shifts("feat", s_feat)

    def stem_store(a, b, value):
        stem_pre[a, b] = value
        halo["stem"].rows[a + 1, b + 1] = silu(value).astype(BF)

    conv(s_feat, w_stem, spans[0], stem_store)

    def pooled(fine, coarse):
        low, up = halo[fine], halo[coarse]
        for a in range(up.w):
            for b in range(up.d):
                cat = [low.rows[2 * a + 1 + i, 2 * b + 1 + j] for i in range(2) for j in range(2)]
                total = mm(cat[0], pool_mean) + mm(cat[1], pool_mean) + mm(cat[2], pool_mean) + mm(cat[3], pool_mean)
                up.rows[a + 1, b + 1] = total.astype(BF)

    pooled("stem", "half")
    halo["half"].start()
    halo["stem"].start()
    halo["cot"].wait()
    stack_shifts("cot", s_cot)
    fb_pool[...] = jnp.zeros(fb_pool.shape, F32)

    def back_store(a, b, value):
        fb_pool[a // 2, b // 2] += value[:f1]
        fb_skip[a, b] = value[f1:]

    conv(s_cot, b_fin, spans[0], back_store)
    halo["half"].wait()
    stack_shifts("half", s_half)

    def mid_store(a, b, value):
        mid_pre[a, b] = value
        halo["mid"].rows[a + 1, b + 1] = silu(value).astype(BF)

    conv(s_half, w_mid, spans[1], mid_store)
    pooled("mid", "quarter")
    halo["quarter"].start()
    halo["mid"].start()
    halo["quarter"].wait()
    stack_shifts("quarter", s_quarter)

    def deep_store(a, b, value):
        deep_pre[a, b] = value
        halo["deep"].rows[a + 1, b + 1] = silu(value).astype(BF)

    conv(s_quarter, w_bot, spans[2], deep_store)
    halo["deep"].start()
    halo["mid"].wait()
    halo["deep"].wait()
    stack_pair("deep", "mid", s_rise)

    def rise_store(a, b, value):
        rise_pre[a, b] = value
        halo["ra"].rows[a + 1, b + 1] = silu(value).astype(BF)
        grad = mm_split(fb_pool[a, b], pool_sum) * slope(value)
        halo["rg"].rows[a + 1, b + 1] = grad.astype(BF)

    conv(s_rise, w_rise, spans[1], rise_store)
    halo["rg"].start()
    halo["ra"].start()
    halo["rg"].wait()
    stack_shifts("rg", s_rg)
    deep_sum = [[None] * spans[2][1] for _ in range(spans[2][0])]

    pair1 = 2 if spans[1][1] % 2 == 0 else 1
    for a in range(spans[1][0]):
        for b in range(0, spans[1][1], pair1):
            result = mm(b_rise[...], patch(s_rg, a, b, pair1))
            for q in range(pair1):
                value = result[:, q * lanes : (q + 1) * lanes]
                rb_skip[a, b + q] = value[f2:]
                at, bt = a // 2, (b + q) // 2
                old = deep_sum[at][bt]
                deep_sum[at][bt] = value[:f2] if old is None else old + value[:f2]
    for a in range(spans[2][0]):
        for b in range(spans[2][1]):
            grad = mm_split(deep_sum[a][b], pool_sum) * slope(deep_pre[a, b])
            halo["dg"].rows[a + 1, b + 1] = grad.astype(BF)
    halo["dg"].start()

    def rise_wgrad(a, b, pair):
        wgrad_into(bases[3], patch(s_rise, a, b, pair), grad_row(halo["rg"].rows, a, b, pair, 1), f1)

    over_rows(spans[1], rise_wgrad)
    halo["dg"].wait()
    stack_shifts("dg", s_dg)

    def quarter_store(a, b, value):
        wide = mm_split(value, spread_mean)
        for i in range(2):
            for j in range(2):
                at, bt = 2 * a + i, 2 * b + j
                grad = (rb_skip[at, bt] + wide) * slope(mid_pre[at, bt])
                halo["mg"].rows[at + 1, bt + 1] = grad.astype(BF)

    conv(s_dg, b_bot, spans[2], quarter_store)
    halo["mg"].start()

    def bottom_wgrad(a, b, pair):
        wgrad_into(bases[2], patch(s_quarter, a, b, pair), grad_row(halo["dg"].rows, a, b, pair, 1), f2)

    over_rows(spans[2], bottom_wgrad)

    def mid_wgrad(a, b, pair):
        wgrad_into(bases[1], patch(s_half, a, b, pair), grad_row(halo["mg"].rows, a, b, pair, 1), f1)

    over_rows(spans[1], mid_wgrad)

    halo["stem"].wait()
    halo["ra"].wait()
    stack_pair("ra", "stem", s_fin)

    def final(a, b, pair):
        cells = patch(s_fin, a, b, pair)
        result = mm(w_fin[...], cells)
        for q in range(pair):
            output[a, b + q] = result[:, q * lanes : (q + 1) * lanes].astype(BF)
        wgrad_into(bases[4], cells, grad_row(cot, a, b, pair, 0), f0)

    over_rows(spans[0], final)

    halo["mg"].wait()
    stack_shifts("mg", s_mg)

    def half_store(a, b, value):
        half_out[a, b] = value
        wide = mm_split(value, spread_mean)
        for i in range(2):
            for j in range(2):
                at, bt = 2 * a + i, 2 * b + j
                grad = (fb_skip[at, bt] + wide) * slope(stem_pre[at, bt])
                stem_grad[at, bt] = grad.astype(BF)

    conv(s_mg, b_mid, spans[1], half_store)

    def stem_wgrad(a, b, pair):
        wgrad_into(bases[0], patch(s_feat, a, b, pair), grad_row(stem_grad, a, b, pair, 0), f0)

    over_rows(spans[0], stem_wgrad)
    for item in halo.values():
        item.finish()


def local(features, cotangent, w_stem, w_middle, w_bottom, w_rise, w_final):
    f0, w, d, h = features.shape
    f1, f2 = w_middle.shape[4], w_bottom.shape[4]
    spans = {0: (w, d), 1: (w // 2, d // 2), 2: (w // 4, d // 4)}
    halos = [(f0, 0), (f0, 0), (f0, 0), (f0, 1), (f1, 1), (f1, 2), (f2, 2), (f1, 1), (f1, 1), (f2, 2), (f1, 1)]
    scratch = [pltpu.SemaphoreType.DMA((27 * len(halos),)), pltpu.SemaphoreType.DMA((27 * len(halos),))]
    for c, level in halos:
        a, b = spans[level]
        scratch += [
            pltpu.VMEM((a + 2, b + 2, c, h), BF),
            pltpu.VMEM((2, 3, 3, c, h), BF),
            pltpu.VMEM((c, h), BF),
        ]
    for c, level in [(f0, 0), (f0, 0), (f0, 1), (f1, 2), (f2 + f1, 1), (f1 + f0, 0), (f1, 1), (f2, 2), (f1, 1)]:
        a, b = spans[level]
        scratch.append(pltpu.VMEM((a + 2, b + 2, 3 * c, h), BF))
    for c, level in [(f0, 0), (f1, 1), (f2, 2), (f1, 1), (f1, 1), (f0, 0), (f1, 1)]:
        scratch.append(pltpu.VMEM((*spans[level], c, h), F32))
    scratch.append(pltpu.VMEM((w, d, f0, h), BF))

    def forward(v):
        return v.reshape(-1, v.shape[4]).T

    def backward(v):
        return v[::-1, ::-1, ::-1].reshape(27, v.shape[3], v.shape[4]).transpose(1, 0, 2).reshape(v.shape[3], -1)

    weights = (w_stem, w_middle, w_bottom, w_rise, w_final)
    total = sum(v.size for v in weights) // h
    vmem = pl.BlockSpec(memory_space=pltpu.VMEM)
    out, grads, half_back = pl.pallas_call(
        functools.partial(step_kernel, (f0, f1, f2, w, d, h)),
        out_shape=(
            jax.ShapeDtypeStruct((w, d, f0, h), BF),
            jax.ShapeDtypeStruct((total, h), F32),
            jax.ShapeDtypeStruct((w // 2, d // 2, f0, h), F32),
        ),
        in_specs=[vmem] * 11,
        out_specs=(vmem,) * 3,
        scratch_shapes=scratch,
        compiler_params=pltpu.CompilerParams(
            collective_id=0, has_side_effects=True, vmem_limit_bytes=60 << 20
        ),
        name="unet_step",
    )(
        features.transpose(1, 2, 0, 3),
        cotangent.transpose(1, 2, 0, 3),
        *[forward(v) for v in weights],
        *[backward(v) for v in weights[1:]],
    )
    summed = reduce_all(grads.astype(BF))
    cells = w * d * h * lax.axis_size("dep") * lax.axis_size("hgt") * lax.axis_size("wid")
    fine, mid, deep = (1.0 / math.sqrt(cells / k) for k in (1.0, 8.0, 64.0))
    results, base = [], 0
    for v, scale in zip(weights, (fine, mid, deep, mid, fine)):
        rows, width = v.size // h, v.shape[4]
        part = summed[base : base + rows].astype(F32) * scale
        base += rows
        part = part.reshape(rows, h // width, width).transpose(1, 0, 2).reshape(v.shape)
        results.append(part)
    return (out.transpose(2, 0, 1, 3), *results, half_back[..., : h // 2].transpose(2, 0, 1, 3))


def reduce_all(grads):
    return lax.psum(grads, ("dep", "hgt", "wid"))


def solution(mesh):
    placed = (P("grp", "wid", "dep", "hgt"), P("grp", "wid", "dep", "hgt"), P(), P(), P(), P(), P())
    grad = P("grp", None, None, None, None)
    return jax.shard_map(
        local,
        mesh=mesh,
        in_specs=placed,
        out_specs=(P("grp", "wid", "dep", "hgt"), grad, grad, grad, grad, grad, P("grp", "wid", "dep", "hgt")),
        check_vma=False,
    )
```

profile of v0, /device:TPU:0, one launch (start us, length us, event | category | flops | bytes accessed | tf_op | source)
XLA Modules:
  0.0 205.4 jit_solution(16626883950407438488)
XLA Ops:
  7.2 0.0 copy-start
  7.2 0.0 all-reduce.2.cloned.1.call-start
  7.2 2.0 copy.55
  9.3 0.1 rev.14
  9.3 0.2 copy.56
  9.5 0.0 copy-start.1
  9.5 1.4 reshape.80
  11.0 1.1 copy.59.refs_9_
  12.2 0.3 copy.58
  12.5 0.9 copy.82
  13.4 0.0 copy-start.4
  13.4 0.1 copy.83
  13.5 0.0 copy-start.6
  13.6 0.0 copy-start.7
  13.6 0.9 reshape.83.refs_7_
  14.5 0.9 reshape.81
  15.4 1.0 copy.54
  16.3 0.8 copy.60.refs_10_
  17.1 0.8 copy.53
  17.9 0.0 copy-done.4
  17.9 0.7 copy.74
  18.7 0.0 copy-done.6
  18.7 0.7 copy_bitcast_fusion.2
  19.4 63.4 %unet_step.1 = (bf16[4,4,32,128]{3,2,1,0:T(8,128)(2,1)}, f32[5616,128]{1,0:T(8,128)}, f32[2,2,32,128]{3,2,1,0:T(8,128)}) custom-call(bf16[4,4,32,128]{3,2,1,0:T(8,128)(2,1)} %get-tuple-element.35.refs_0_, bf16[4,4,32,128]{3,2,1,0:T(8,128)(2,1)} %get-tuple-element.34.refs_1_, bf16[32,864]{1,0:T(8,128)(2,1)} %bitcast.78, bf16[64,864]{1,0:T(8,128)(2,1)} %bitcast.75, ...), custom_call_target="tpu_custom_call" | custom-call | tf_op jit(solution)/shard_map/unet_step/pallas_call | solution.py:436
  82.8 3.0 %convert_element_type.18 = bf16[5616,128]{1,0:T(8,128)(2,1)} convert(f32[5616,128]{1,0:T(8,128)} %get-tuple-element.11) | non-fusion elementwise | flops 718848 | bytes 4313088 | tf_op jit(solution)/shard_map/convert_element_type | solution.py:456
  85.8 0.0 all-reduce.2.cloned.1.call-update
  85.9 0.9 copy-done.5
  86.7 0.7 copy.69
  87.5 0.0 copy-done.8
  87.5 0.7 copy.73
  88.2 92.8 %all-reduce.2.cloned.1.call-done = bf16[5616,128]{1,0:T(8,128)(2,1)} async-done(((bf16[5616,128]{1,0:T(8,128)(2,1)}), bf16[5616,128]{1,0:T(8,128)(2,1)}) %all-reduce.2.cloned.1.call-update) | async-done | bytes 1437712 | tf_op jit(solution)/shard_map/psum | solution.py:470
  181.0 1.2 convert_multiply_fusion
  182.2 0.4 copy.65
  182.6 2.1 %copy.66 = f32[2,2592,64]{1,0,2:T(2,128)} copy(f32[2,2592,64]{1,2,0:T(8,128)S(1)} %bitcast.58) | data formatting | bytes 2654208 | tf_op jit(solution)/shard_map/transpose | solution.py:464
  184.7 3.6 %reshape.95 = f32[3,3,3,192,64]{3,2,1,0,4:T(4,128)S(1)} reshape(f32[2,2592,64]{1,0,2:T(2,128)} %copy.66) | data formatting | bytes 2654208 | tf_op jit(solution)/shard_map/reshape | solution.py:464
  188.4 1.5 copy.71
  189.9 0.9 convert_multiply_fusion.2
  190.8 0.2 copy.67
  191.0 0.3 copy.68
  191.3 0.6 reshape.97
  191.8 0.8 copy.72
  192.7 0.9 convert_multiply_fusion.3
  193.6 0.1 copy.63
  193.7 1.0 copy.64
  194.7 0.8 convert_multiply_fusion.4
  195.5 0.1 copy.61
  195.6 1.0 copy.75
  196.6 2.0 convert_multiply_fusion.1
  (13 shorter events, 0.1 us)
Async XLA Ops:
  7.2 2.1 %copy-start = (bf16[3,3,3,192,64]{3,4,2,1,0:T(8,128)(2,1)S(1)}, bf16[3,3,3,192,64]{3,4,2,1,0:T(8,128)(2,1)}, u32[]{:S(2)}) copy-start(bf16[3,3,3,192,64]{3,4,2,1,0:T(8,128)(2,1)} %param.12) | copy-start | bytes 1990660
  7.2 2.1 %copy-start.2 = (bf16[3,3,3,96,32]{3,4,2,1,0:T(8,128)(2,1)S(1)}, bf16[3,3,3,96,32]{3,4,2,1,0:T(8,128)(2,1)}, u32[]{:S(2)}) copy-start(bf16[3,3,3,96,32]{3,4,2,1,0:T(8,128)(2,1)} %param.13) | copy-start | bytes 497668
  7.2 173.8 %all-reduce.2.cloned.1.call-start = ((), (), s32[]{:S(2)}) async-start(), calls=%async_computation | async-start | bytes 2875392 | tf_op jit(solution)/shard_map/psum | solution.py:470
  9.5 2.6 %copy-start.1 = (bf16[3,3,3,64,128]{4,3,2,1,0:T(8,128)(2,1)S(1)}, bf16[3,3,3,64,128]{4,3,2,1,0:T(8,128)(2,1)}, u32[]{:S(2)}) copy-start(bf16[3,3,3,64,128]{4,3,2,1,0:T(8,128)(2,1)} %param.11) | copy-start | bytes 1327108
  12.1 1.3 copy-start.3
  13.4 4.5 %copy-start.4 = (bf16[3,3,3,32,32]{4,3,2,1,0:T(8,128)(2,1)S(1)}, bf16[3,3,3,32,32]{4,3,2,1,0:T(8,128)(2,1)}, u32[]{:S(2)}) copy-start(bf16[3,3,3,32,32]{4,3,2,1,0:T(8,128)(2,1)} %param.9) | copy-start | bytes 165892
  13.5 5.1 %copy-start.6 = (bf16[32,4,4,128]{3,2,1,0:T(4,128)(2,1)S(1)}, bf16[32,4,4,128]{3,2,1,0:T(4,128)(2,1)}, u32[]{:S(2)}) copy-start(bf16[32,4,4,128]{3,2,1,0:T(4,128)(2,1)} %param.8) | copy-start | bytes 393220
  13.6 5.1 %copy-start.7 = (bf16[32,4,4,128]{3,2,1,0:T(4,128)(2,1)S(1)}, bf16[32,4,4,128]{3,2,1,0:T(4,128)(2,1)}, u32[]{:S(2)}) copy-start(bf16[32,4,4,128]{3,2,1,0:T(4,128)(2,1)} %param.7) | copy-start | bytes 393220
  85.8 0.9 copy-start.5
  85.8 1.6 copy-start.8
Sparse Core Ops, SparseCore 0:
  86.0 94.9 all-reduce.1
where the time goes:
time: 206 us; the launch traced here: 205 us
  waiting for transfers between devices  92.8 us (45%)
  Pallas kernels  63.4 us (31%)
  local copies, waits for them, and re-layouts  26 us (13%)
  between operations  14.2 us (7%)
  other arithmetic  8.9 us (4%)
    psum x1, waiting for transfers between devices, reduce_all(): return lax.psum(grads, ('dep', 'hgt', 'wid'))  92.8 us
    pallas_call x1, Pallas kernels, local(): pl.pallas_call(functools.partial(step_kernel, (f0, f1, f2, w, d, h)), out...  63.4 us
    unnamed x26, local copies, waits for them, and re-layouts  8.72 us
    mul x5, other arithmetic, local(): part = summed[base:base + rows].astype(F32) * scale  5.85 us
    reshape x5, local copies, waits for them, and re-layouts, forward(): return v.reshape(-1, v.shape[4]).T  4.83 us
    reshape x2, local copies, waits for them, and re-layouts, local(): part.reshape(rows, h // width, width).transpose(1, 0, 2).reshape(v.shape)  4.2 us
  transfers between devices with their start and end apart: 1, of which 1 were waited for; matrix products, arithmetic and copies ran while one was open for 1% of the time, Pallas kernels for 0%

commit v1 on v0

--- a/solution.py
+++ b/solution.py
@@ -9,6 +9,7 @@
 from jax.sharding import PartitionSpec as P
 
 BF, F32 = jnp.bfloat16, jnp.float32
+SEGMENTS = ((3, 4), (2, 1), (0,))
 AXES = ("grp", "dep", "hgt", "wid")
 
 
@@ -148,12 +149,93 @@
         return before.astype(BF), row, after.astype(BF)
 
 
+def at(name, position):
+    return {n: position if n == name else lax.axis_index(n) for n in ("dep", "hgt", "wid")}
+
+
+class Summed:
+    order = ("wid", "hgt", "dep")
+
+    def __init__(self, full, buffers, send, recv):
+        self.total = buffers[0]
+        self.levels = [(buffers[0], buffers[1], buffers[2]), buffers[3:6], buffers[6:9]]
+        self.full, self.send, self.recv = full, send, recv
+        self.stage, self.open, self.sent = 0, [], []
+
+    def exchange(self, stage, name, pieces):
+        i, n = lax.axis_index(name), lax.axis_size(name)
+        self.open = []
+        for k in range(1, n):
+            source, dest = pieces(lax.rem(i + k, n), i)
+            copy = pltpu.make_async_remote_copy(
+                src_ref=source,
+                dst_ref=dest,
+                send_sem=self.send.at[stage, k],
+                recv_sem=self.recv.at[stage, k],
+                device_id=at(name, lax.rem(i + k, n)),
+                device_id_type=pl.DeviceIdType.MESH,
+            )
+            copy.start()
+            self.open.append(copy)
+            self.sent.append(copy)
+
+    def arrive(self):
+        for copy in self.open:
+            copy.wait_recv()
+        self.open = []
+
+    def step(self):
+        stage = self.stage
+        self.stage += 1
+        if stage > 0:
+            self.arrive()
+        if 0 < stage <= 3:
+            name = self.order[stage - 1]
+            i, n = lax.axis_index(name), lax.axis_size(name)
+            held, _, came = self.levels[stage - 1]
+            m = held.shape[0] // n
+            value = held[part(i, m)]
+            for k in range(1, n):
+                value = value + came[part(lax.rem(i + k, n), m)].astype(F32)
+            if stage < 3:
+                self.levels[stage][0][...] = value
+            else:
+                place = 0
+                for axis in self.order:
+                    place = place * lax.axis_size(axis) + lax.axis_index(axis)
+                self.full[part(place, m)] = value.astype(BF)
+        if stage < 3:
+            held, wire, came = self.levels[stage]
+            m = held.shape[0] // lax.axis_size(self.order[stage])
+            wire[...] = held[...].astype(BF)
+            self.exchange(stage, self.order[stage], lambda to, me: (wire.at[part(to, m)], came.at[part(me, m)]))
+        elif stage < 6:
+            depth = 6 - stage
+            place, count = 0, 1
+            for axis in self.order[:depth]:
+                place = place * lax.axis_size(axis) + lax.axis_index(axis)
+                count *= lax.axis_size(axis)
+            m = self.full.shape[0] // count
+            piece = self.full.at[part(place, m)]
+            self.exchange(stage, self.order[depth - 1], lambda to, me: (piece, piece))
+
+    def finish(self):
+        while self.stage < 7:
+            self.step()
+        for copy in self.sent:
+            copy.wait_send()
+
+
+def part(i, m):
+    return pl.ds(pl.multiple_of(i * m, 16), m)
+
+
 def step_kernel(cfg, *refs):
     (f0, f1, f2, w, d, h) = cfg
     (feat, cot, w_stem, w_mid, w_bot, w_rise, w_fin, b_mid, b_bot, b_rise, b_fin) = refs[:11]
-    (output, grads, half_out) = refs[11:14]
+    (output, full0, full1, full2, half_out) = refs[11:16]
     names = ("feat", "cot", "stem", "half", "mid", "quarter", "deep", "ra", "rg", "dg", "mg")
-    refs = refs[14:]
+    refs = refs[16:]
     spans = {0: (w, d, h), 1: (w // 2, d // 2, h // 2), 2: (w // 4, d // 4, h // 4)}
     levels = dict(feat=0, cot=0, stem=0, half=1, mid=1, quarter=2, deep=2, ra=1, rg=1, dg=2, mg=1)
     send, recv = refs[0], refs[1]
@@ -163,7 +245,12 @@
         halo[name] = Halo(i, rows, edges, own, spans[levels[name]], (send, recv))
     rest = refs[2 + 3 * len(names) :]
     (s_feat, s_cot, s_half, s_quarter, s_rise, s_fin, s_rg, s_dg, s_mg) = rest[:9]
-    (stem_pre, mid_pre, deep_pre, rise_pre, fb_pool, fb_skip, rb_skip, stem_grad) = rest[9:]
+    (stem_pre, mid_pre, deep_pre, rise_pre, fb_pool, fb_skip, rb_skip, stem_grad) = rest[9:17]
+    rest = rest[17:]
+    sums = [
+        Summed(full, rest[11 * i : 11 * i + 9], rest[11 * i + 9], rest[11 * i + 10])
+        for i, full in enumerate((full0, full1, full2))
+    ]
 
     for item in halo.values():
         item.rows[...] = jnp.zeros(item.rows.shape, BF)
@@ -181,11 +268,25 @@
                 pl.semaphore_signal, barrier, 1, device_id=target, device_id_type=pl.DeviceIdType.MESH
             ),
         )
+    others = 0
+    for name in ("dep", "hgt"):
+        i, n = lax.axis_index(name), lax.axis_size(name)
+        for k in range(1, n):
+            other = lax.rem(i + k, n)
+            far = jnp.logical_or(other - i > 1, i - other > 1)
+            if n > 2:
+                Halo.guarded(
+                    [far],
+                    functools.partial(
+                        pl.semaphore_signal, barrier, 1, device_id=at(name, other), device_id_type=pl.DeviceIdType.MESH
+                    ),
+                )
+        others = others + n - (1 + jnp.minimum(i, 1) + jnp.minimum(n - 1 - i, 1))
     peers = 1
     for name in ("wid", "dep", "hgt"):
         i, n = lax.axis_index(name), lax.axis_size(name)
         peers = peers * (1 + jnp.minimum(i, 1) + jnp.minimum(n - 1 - i, 1))
-    pl.semaphore_wait(barrier, peers - 1)
+    pl.semaphore_wait(barrier, peers - 1 + others)
 
     lanes = h
     pool = pattern(lanes, lambda r, c: r // 2 == c)
@@ -246,16 +347,19 @@
             pieces = [jnp.zeros_like(grad)] * groups
             pieces[g] = grad
             full = pieces[0] if groups == 1 else jnp.concatenate(pieces, axis=0)
-            part = mm_nt(patches[g * count : (g + 1) * count], full)
-            grads[base : base + count] += part
+            value = mm_nt(patches[g * count : (g + 1) * count], full)
+            where = sums[base[0]].total
+            where[base[1] : base[1] + count] += value
 
     def grad_row(ref, a, b, pair, pad):
         parts = [ref[a + pad, b + pad + q] for q in range(pair)]
         return parts[0] if pair == 1 else jnp.concatenate(parts, axis=1)
 
     sizes = [27 * f0 * f0, 27 * f0 * f1, 27 * f1 * f2, 27 * (f2 + f1) * f1, 27 * (f1 + f0) * f0]
-    bases = [sum(sizes[:i]) // lanes for i in range(5)]
-    grads[...] = jnp.zeros(grads.shape, F32)
+    rows_of = [v // lanes for v in sizes]
+    bases = {i: (seg, sum(rows_of[j] for j in SEGMENTS[seg][: SEGMENTS[seg].index(i)])) for seg in range(3) for i in SEGMENTS[seg]}
+    for item in sums:
+        item.total[...] = jnp.zeros(item.total.shape, F32)
 
     halo["feat"].start()
     halo["cot"].start()
@@ -332,9 +436,9 @@
             for q in range(pair1):
                 value = result[:, q * lanes : (q + 1) * lanes]
                 rb_skip[a, b + q] = value[f2:]
-                at, bt = a // 2, (b + q) // 2
-                old = deep_sum[at][bt]
-                deep_sum[at][bt] = value[:f2] if old is None else old + value[:f2]
+                ap, bt = a // 2, (b + q) // 2
+                old = deep_sum[ap][bt]
+                deep_sum[ap][bt] = value[:f2] if old is None else old + value[:f2]
     for a in range(spans[2][0]):
         for b in range(spans[2][1]):
             grad = mm_split(deep_sum[a][b], pool_sum) * slope(deep_pre[a, b])
@@ -345,30 +449,6 @@
         wgrad_into(bases[3], patch(s_rise, a, b, pair), grad_row(halo["rg"].rows, a, b, pair, 1), f1)
 
     over_rows(spans[1], rise_wgrad)
-    halo["dg"].wait()
-    stack_shifts("dg", s_dg)
-
-    def quarter_store(a, b, value):
-        wide = mm_split(value, spread_mean)
-        for i in range(2):
-            for j in range(2):
-                at, bt = 2 * a + i, 2 * b + j
-                grad = (rb_skip[at, bt] + wide) * slope(mid_pre[at, bt])
-                halo["mg"].rows[at + 1, bt + 1] = grad.astype(BF)
-
-    conv(s_dg, b_bot, spans[2], quarter_store)
-    halo["mg"].start()
-
-    def bottom_wgrad(a, b, pair):
-        wgrad_into(bases[2], patch(s_quarter, a, b, pair), grad_row(halo["dg"].rows, a, b, pair, 1), f2)
-
-    over_rows(spans[2], bottom_wgrad)
-
-    def mid_wgrad(a, b, pair):
-        wgrad_into(bases[1], patch(s_half, a, b, pair), grad_row(halo["mg"].rows, a, b, pair, 1), f1)
-
-    over_rows(spans[1], mid_wgrad)
-
     halo["stem"].wait()
     halo["ra"].wait()
     stack_pair("ra", "stem", s_fin)
@@ -381,7 +461,32 @@
         wgrad_into(bases[4], cells, grad_row(cot, a, b, pair, 0), f0)
 
     over_rows(spans[0], final)
-
+    sums[0].step()
+    halo["dg"].wait()
+    stack_shifts("dg", s_dg)
+
+    def quarter_store(a, b, value):
+        wide = mm_split(value, spread_mean)
+        for i in range(2):
+            for j in range(2):
+                at_, bt = 2 * a + i, 2 * b + j
+                grad = (rb_skip[at_, bt] + wide) * slope(mid_pre[at_, bt])
+                halo["mg"].rows[at_ + 1, bt + 1] = grad.astype(BF)
+
+    conv(s_dg, b_bot, spans[2], quarter_store)
+    halo["mg"].start()
+    sums[0].step()
+
+    def bottom_wgrad(a, b, pair):
+        wgrad_into(bases[2], patch(s_quarter, a, b, pair), grad_row(halo["dg"].rows, a, b, pair, 1), f2)
+
+    over_rows(spans[2], bottom_wgrad)
+
+    def mid_wgrad(a, b, pair):
+        wgrad_into(bases[1], patch(s_half, a, b, pair), grad_row(halo["mg"].rows, a, b, pair, 1), f1)
+
+    over_rows(spans[1], mid_wgrad)
+    sums[1].step()
     halo["mg"].wait()
     stack_shifts("mg", s_mg)
 
@@ -390,16 +495,26 @@
         wide = mm_split(value, spread_mean)
         for i in range(2):
             for j in range(2):
-                at, bt = 2 * a + i, 2 * b + j
-                grad = (fb_skip[at, bt] + wide) * slope(stem_pre[at, bt])
-                stem_grad[at, bt] = grad.astype(BF)
+                at_, bt = 2 * a + i, 2 * b + j
+                grad = (fb_skip[at_, bt] + wide) * slope(stem_pre[at_, bt])
+                stem_grad[at_, bt] = grad.astype(BF)
 
     conv(s_mg, b_mid, spans[1], half_store)
+    sums[0].step()
+    sums[1].step()
 
     def stem_wgrad(a, b, pair):
         wgrad_into(bases[0], patch(s_feat, a, b, pair), grad_row(stem_grad, a, b, pair, 0), f0)
 
     over_rows(spans[0], stem_wgrad)
+    sums[2].step()
+    sums[0].step()
+    sums[1].step()
+    for _ in range(3):
+        for item in (sums[2], sums[0], sums[1]):
+            item.step()
+    for item in (sums[2], sums[0], sums[1]):
+        item.finish()
     for item in halo.values():
         item.finish()
 
@@ -423,6 +538,17 @@
     for c, level in [(f0, 0), (f1, 1), (f2, 2), (f1, 1), (f1, 1), (f0, 0), (f1, 1)]:
         scratch.append(pltpu.VMEM((*spans[level], c, h), F32))
     scratch.append(pltpu.VMEM((w, d, f0, h), BF))
+    weights = (w_stem, w_middle, w_bottom, w_rise, w_final)
+    counts = [lax.axis_size(axis) for axis in Summed.order]
+    unit = 16 * math.prod(counts)
+    lengths = []
+    for members in SEGMENTS:
+        rows = -(-sum(weights[i].size // h for i in members) // unit) * unit
+        lengths.append(rows)
+        for n in counts:
+            scratch += [pltpu.VMEM((rows, h), F32), pltpu.VMEM((rows, h), BF), pltpu.VMEM((rows, h), BF)]
+            rows //= n
+        scratch += [pltpu.SemaphoreType.DMA((6, max(counts))), pltpu.SemaphoreType.DMA((6, max(counts)))]
 
     def forward(v):
         return v.reshape(-1, v.shape[4]).T
@@ -430,18 +556,16 @@
     def backward(v):
         return v[::-1, ::-1, ::-1].reshape(27, v.shape[3], v.shape[4]).transpose(1, 0, 2).reshape(v.shape[3], -1)
 
-    weights = (w_stem, w_middle, w_bottom, w_rise, w_final)
-    total = sum(v.size for v in weights) // h
     vmem = pl.BlockSpec(memory_space=pltpu.VMEM)
-    out, grads, half_back = pl.pallas_call(
+    out, *packed, half_back = pl.pallas_call(
         functools.partial(step_kernel, (f0, f1, f2, w, d, h)),
         out_shape=(
             jax.ShapeDtypeStruct((w, d, f0, h), BF),
-            jax.ShapeDtypeStruct((total, h), F32),
+            *[jax.ShapeDtypeStruct((rows, h), BF) for rows in lengths],
             jax.ShapeDtypeStruct((w // 2, d // 2, f0, h), F32),
         ),
         in_specs=[vmem] * 11,
-        out_specs=(vmem,) * 3,
+        out_specs=(vmem,) * 5,
         scratch_shapes=scratch,
         compiler_params=pltpu.CompilerParams(
             collective_id=0, has_side_effects=True, vmem_limit_bytes=60 << 20
@@ -453,21 +577,32 @@
         *[forward(v) for v in weights],
         *[backward(v) for v in weights[1:]],
     )
-    summed = reduce_all(grads.astype(BF))
     cells = w * d * h * lax.axis_size("dep") * lax.axis_size("hgt") * lax.axis_size("wid")
     fine, mid, deep = (1.0 / math.sqrt(cells / k) for k in (1.0, 8.0, 64.0))
-    results, base = [], 0
-    for v, scale in zip(weights, (fine, mid, deep, mid, fine)):
-        rows, width = v.size // h, v.shape[4]
-        part = summed[base : base + rows].astype(F32) * scale
-        base += rows
-        part = part.reshape(rows, h // width, width).transpose(1, 0, 2).reshape(v.shape)
-        results.append(part)
+    scales = (fine, mid, deep, mid, fine)
+
+    def unpack(*refs):
+        for members, source in zip(SEGMENTS, refs[:3]):
+            base = 0
+            for i in members:
+                target = refs[3 + i]
+                width = target.shape[1]
+                rows = target.shape[0] * width // h
+                value = source[base : base + rows].astype(F32) * scales[i]
+                base += rows
+                for g in range(h // width):
+                    target[g * rows : (g + 1) * rows] = value[:, g * width : (g + 1) * width]
+
+    flat = pl.pallas_call(
+        unpack,
+        out_shape=tuple(jax.ShapeDtypeStruct((v.size // v.shape[4], v.shape[4]), F32) for v in weights),
+        in_specs=[vmem] * 3,
+        out_specs=(vmem,) * 5,
+        compiler_params=pltpu.CompilerParams(vmem_limit_bytes=32 << 20),
+        name="unpack",
+    )(*packed)
+    results = [r.reshape(v.shape) for r, v in zip(flat, weights)]
     return (out.transpose(2, 0, 1, 3), *results, half_back[..., : h // 2].transpose(2, 0, 1, 3))
-
-
-def reduce_all(grads):
-    return lax.psum(grads, ("dep", "hgt", "wid"))
 
 
 def solution(mesh):

time: 206 us -> 122 us (0.59)
  waiting for transfers between devices: 92.8 us -> 0 us
  Pallas kernels: 63.4 us -> 95 us
  between operations: 14.2 us -> 0.72 us
  other arithmetic: 8.9 us -> 0 us
    psum x1 -> x0, waiting for transfers between devices: 92.8 us -> none  [reduce_all(): return lax.psum(grads, ('dep', 'hgt', 'wid'))]
    pallas_call x1, Pallas kernels: 63.4 us -> 93 us  [local(): pl.pallas_call(functools.partial(step_kernel, (f0, f1, f2, w, d, h)), out...]
    mul x5 -> x0, other arithmetic: 5.85 us -> none  [local(): part = summed[base:base + rows].astype(F32) * scale]
    unnamed x26 -> x25, local copies, waits for them, and re-layouts: 8.72 us -> 13 us
    reshape x2 -> x0, local copies, waits for them, and re-layouts: 4.2 us -> none  [local(): part.reshape(rows, h // width, width).transpose(1, 0, 2).reshape(v.shape)]
    transpose x3 -> x0, local copies, waits for them, and re-layouts: 3.35 us -> none  [local(): part.reshape(rows, h // width, width).transpose(1, 0, 2).reshape(v.shape)]
    convert_element_type x1 -> x0, other arithmetic: 3.05 us -> none  [local(): summed = reduce_all(grads.astype(BF))]
  transfers between devices with their start and end apart: 1 -> 0, of which waited for: 1 -> 0; matrix products, arithmetic and copies ran while one was open for 1% -> 0% of each run, Pallas kernels for 0% -> 0%
where the time goes in v1:
time: 122 us; the launch traced here: 121 us
  Pallas kernels  95 us (78%)
  local copies, waits for them, and re-layouts  25.7 us (21%)
    pallas_call x1, Pallas kernels, local(): pl.pallas_call(functools.partial(step_kernel, (f0, f1, f2, w, d, h)), out...  93 us
    unnamed x25, local copies, waits for them, and re-layouts  13 us
    reshape x5, local copies, waits for them, and re-layouts, forward(): return v.reshape(-1, v.shape[4]).T  6.75 us
    reshape x5, local copies, waits for them, and re-layouts, backward(): v[::-1, ::-1, ::-1].reshape(27, v.shape[3], v.shape[4]).transpose(1, 0, 2)  3.24 us

profile of v1, /device:TPU:0, one launch (start us, length us, event | category | flops | bytes accessed | tf_op | source)
XLA Modules:
  0.0 121.4 jit_solution(15156057468948860265)
XLA Ops:
  0.6 0.0 copy-start.6
  0.6 0.0 copy-start.7
  0.7 0.0 copy-start.8
  0.7 1.7 %copy.44 = bf16[864,32]{0,1:T(8,128)(2,1)} copy(bf16[864,32]{1,0:T(8,128)(2,1)} %bitcast.60) | data formatting | bytes 110592 | tf_op jit(solution)/shard_map/reshape | solution.py:554
  2.4 1.7 %copy.32 = bf16[864,64]{0,1:T(8,128)(2,1)} copy(bf16[864,64]{1,0:T(8,128)(2,1)} %bitcast.55) | data formatting | bytes 221184 | tf_op jit(solution)/shard_map/reshape | solution.py:554
  4.1 0.0 copy-start.5
  4.1 1.0 rev.12
  5.1 0.1 copy.51
  5.2 0.9 reshape.74.refs_7_
  6.1 0.0 copy-done.6
  6.1 0.8 copy.39.refs_10_
  6.9 0.0 copy-done.7
  6.9 0.0 copy-done.8
  6.9 0.8 copy_bitcast_fusion.2
  7.7 0.2 copy.35
  7.8 0.9 reshape.72
  8.7 0.0 copy-done.5
  8.7 0.0 copy-start.4
  8.8 0.3 copy.37
  9.1 0.9 copy.50
  10.0 1.0 copy.33
  11.0 0.0 copy-done.4
  11.0 0.1 rev.14
  11.1 1.1 copy.38.refs_9_
  12.3 0.8 copy.34
  13.0 1.4 %reshape.71 = bf16[5184,64]{0,1:T(8,128)(2,1)} reshape(bf16[3,3,3,192,64]{3,2,1,0,4:T(4,128)(2,1)S(1)} %copy.34) | data formatting | bytes 1327104 | tf_op jit(solution)/shard_map/reshape | solution.py:554
  14.5 93.0 %unet_step.1 = (bf16[4,4,32,128]{3,2,1,0:T(8,128)(2,1)}, bf16[3328,128]{1,0:T(8,128)(2,1)}, bf16[2304,128]{1,0:T(8,128)(2,1)}, bf16[256,128]{1,0:T(8,128)(2,1)}, f32[2,2,32,128]{3,2,1,0:T(8,128)}) custom-call(bf16[4,4,32,128]{3,2,1,0:T(8,128)(2,1)} %get-tuple-element.42.refs_0_, bf16[4,4,32,128]{3,2,1,0:T(8,128)(2,1)} %get-tuple-element.41.refs_1_, ...), custom_call_target="tpu_custom_call" | custom-call | tf_op jit(solution)/shard_map/unet_step/pallas_call | solution.py:560
  107.5 1.6 %copy.40 = bf16[32,4,4,128]{3,2,1,0:T(4,128)(2,1)} copy(bf16[32,4,4,128]{3,0,2,1:T(8,128)(2,1)} %bitcast.61) | data formatting | bytes 262144
  109.1 0.8 slice_bitcast_fusion
  110.0 0.7 copy.43
  110.7 0.0 copy-start.1
  110.7 1.2 copy-done.1
  111.8 0.0 copy-start.2
  111.8 1.1 copy-done.2
  112.9 0.0 copy-start.3
  112.9 0.8 copy-done.3
  113.7 1.9 %unpack.1 = (f32[864,32]{1,0:T(8,128)}, f32[864,64]{1,0:T(8,128)}, f32[1728,128]{1,0:T(8,128)}, f32[5184,64]{1,0:T(8,128)S(1)}, f32[2592,32]{1,0:T(8,128)S(1)}) custom-call(bf16[3328,128]{1,0:T(8,128)(2,1)S(1)} %copy-done.1, bf16[2304,128]{1,0:T(8,128)(2,1)S(1)} %copy-done.2, bf16[256,128]{1,0:T(8,128)(2,1)S(1)} %copy-done.3), custom_call_target="tpu_custom_call" | custom-call | tf_op jit(solution)/shard_map/unpack/pallas_call | solution.py:596
  115.6 0.0 copy-start
  115.6 1.1 copy-done
  116.7 2.5 %copy.42 = f32[3,3,3,96,32]{3,4,2,1,0:T(8,128)} copy(f32[3,3,3,96,32]{4,3,2,1,0:T(8,128)} %bitcast.45) | data formatting | bytes 663552
  119.2 2.2 %copy.41 = f32[3,3,3,192,64]{3,4,2,1,0:T(8,128)} copy(f32[3,3,3,192,64]{4,3,2,1,0:T(8,128)S(1)} %bitcast.44) | data formatting | bytes 2654208
  (2 shorter events, 0.0 us)
Async XLA Ops:
  0.6 5.5 %copy-start.6 = (bf16[3,3,3,96,32]{3,4,2,1,0:T(8,128)(2,1)S(1)}, bf16[3,3,3,96,32]{3,4,2,1,0:T(8,128)(2,1)}, u32[]{:S(2)}) copy-start(bf16[3,3,3,96,32]{3,4,2,1,0:T(8,128)(2,1)} %param.13) | copy-start | bytes 497668
  0.6 6.3 %copy-start.7 = (bf16[32,4,4,128]{3,2,1,0:T(4,128)(2,1)S(1)}, bf16[32,4,4,128]{3,2,1,0:T(4,128)(2,1)}, u32[]{:S(2)}) copy-start(bf16[32,4,4,128]{3,2,1,0:T(4,128)(2,1)} %param.8) | copy-start | bytes 393220
  0.7 6.3 %copy-start.8 = (bf16[32,4,4,128]{3,2,1,0:T(4,128)(2,1)S(1)}, bf16[32,4,4,128]{3,2,1,0:T(4,128)(2,1)}, u32[]{:S(2)}) copy-start(bf16[32,4,4,128]{3,2,1,0:T(4,128)(2,1)} %param.7) | copy-start | bytes 393220
  4.1 4.6 %copy-start.5 = (bf16[3,3,3,64,128]{4,3,2,1,0:T(8,128)(2,1)S(1)}, bf16[3,3,3,64,128]{4,3,2,1,0:T(8,128)(2,1)}, u32[]{:S(2)}) copy-start(bf16[3,3,3,64,128]{4,3,2,1,0:T(8,128)(2,1)} %param.11) | copy-start | bytes 1327108
  8.7 2.3 %copy-start.4 = (bf16[3,3,3,192,64]{3,4,2,1,0:T(8,128)(2,1)S(1)}, bf16[3,3,3,192,64]{3,4,2,1,0:T(8,128)(2,1)}, u32[]{:S(2)}) copy-start(bf16[3,3,3,192,64]{3,4,2,1,0:T(8,128)(2,1)} %param.12) | copy-start | bytes 1990660
  110.7 1.2 copy-start.1
  111.8 1.1 copy-start.2
  112.9 0.8 copy-start.3
  115.6 1.1 copy-start

commit v2 on v1

--- a/solution.py
+++ b/solution.py
@@ -9,7 +9,7 @@
 from jax.sharding import PartitionSpec as P
 
 BF, F32 = jnp.bfloat16, jnp.float32
-SEGMENTS = ((3, 4), (2, 1), (0,))
+SEGMENTS = ((3,), (2, 4), (1, 0))
 AXES = ("grp", "dep", "hgt", "wid")
 
 
@@ -232,10 +232,10 @@
 
 def step_kernel(cfg, *refs):
     (f0, f1, f2, w, d, h) = cfg
-    (feat, cot, w_stem, w_mid, w_bot, w_rise, w_fin, b_mid, b_bot, b_rise, b_fin) = refs[:11]
-    (output, full0, full1, full2, half_out) = refs[11:16]
+    (feat, cot, raw_stem, raw_mid, raw_bot, w_rise, w_fin, b_rise, b_fin) = refs[:9]
+    (output, full0, full1, full2, half_out) = refs[9:14]
     names = ("feat", "cot", "stem", "half", "mid", "quarter", "deep", "ra", "rg", "dg", "mg")
-    refs = refs[16:]
+    refs = refs[14:]
     spans = {0: (w, d, h), 1: (w // 2, d // 2, h // 2), 2: (w // 4, d // 4, h // 4)}
     levels = dict(feat=0, cot=0, stem=0, half=1, mid=1, quarter=2, deep=2, ra=1, rg=1, dg=2, mg=1)
     send, recv = refs[0], refs[1]
@@ -246,7 +246,8 @@
     rest = refs[2 + 3 * len(names) :]
     (s_feat, s_cot, s_half, s_quarter, s_rise, s_fin, s_rg, s_dg, s_mg) = rest[:9]
     (stem_pre, mid_pre, deep_pre, rise_pre, fb_pool, fb_skip, rb_skip, stem_grad) = rest[9:17]
-    rest = rest[17:]
+    (w_stem, w_mid, w_bot, b_mid, b_bot) = rest[17:22]
+    rest = rest[22:]
     sums = [
         Summed(full, rest[11 * i : 11 * i + 9], rest[11 * i + 9], rest[11 * i + 10])
         for i, full in enumerate((full0, full1, full2))
@@ -363,6 +364,12 @@
 
     halo["feat"].start()
     halo["cot"].start()
+    for raw, target in ((raw_stem, w_stem), (raw_mid, w_mid), (raw_bot, w_bot)):
+        target[...] = raw[...].reshape(-1, raw.shape[2]).T
+    for raw, target in ((raw_mid, b_mid), (raw_bot, b_bot)):
+        taps, _, width = raw.shape
+        for k in range(taps):
+            target[:, k * width : (k + 1) * width] = raw[taps - 1 - k]
     halo["feat"].wait()
     stack_shifts("feat", s_feat)
 
@@ -425,6 +432,12 @@
     conv(s_rise, w_rise, spans[1], rise_store)
     halo["rg"].start()
     halo["ra"].start()
+
+    def rise_wgrad(a, b, pair):
+        wgrad_into(bases[3], patch(s_rise, a, b, pair), grad_row(halo["rg"].rows, a, b, pair, 1), f1)
+
+    over_rows(spans[1], rise_wgrad)
+    sums[0].step()
     halo["rg"].wait()
     stack_shifts("rg", s_rg)
     deep_sum = [[None] * spans[2][1] for _ in range(spans[2][0])]
@@ -445,10 +458,11 @@
             halo["dg"].rows[a + 1, b + 1] = grad.astype(BF)
     halo["dg"].start()
 
-    def rise_wgrad(a, b, pair):
-        wgrad_into(bases[3], patch(s_rise, a, b, pair), grad_row(halo["rg"].rows, a, b, pair, 1), f1)
-
-    over_rows(spans[1], rise_wgrad)
+    def bottom_wgrad(a, b, pair):
+        wgrad_into(bases[2], patch(s_quarter, a, b, pair), grad_row(halo["dg"].rows, a, b, pair, 1), f2)
+
+    over_rows(spans[2], bottom_wgrad)
+    sums[0].step()
     halo["stem"].wait()
     halo["ra"].wait()
     stack_pair("ra", "stem", s_fin)
@@ -461,6 +475,7 @@
         wgrad_into(bases[4], cells, grad_row(cot, a, b, pair, 0), f0)
 
     over_rows(spans[0], final)
+    sums[1].step()
     sums[0].step()
     halo["dg"].wait()
     stack_shifts("dg", s_dg)
@@ -475,18 +490,15 @@
 
     conv(s_dg, b_bot, spans[2], quarter_store)
     halo["mg"].start()
+    sums[1].step()
     sums[0].step()
-
-    def bottom_wgrad(a, b, pair):
-        wgrad_into(bases[2], patch(s_quarter, a, b, pair), grad_row(halo["dg"].rows, a, b, pair, 1), f2)
-
-    over_rows(spans[2], bottom_wgrad)
 
     def mid_wgrad(a, b, pair):
         wgrad_into(bases[1], patch(s_half, a, b, pair), grad_row(halo["mg"].rows, a, b, pair, 1), f1)
 
     over_rows(spans[1], mid_wgrad)
     sums[1].step()
+    sums[0].step()
     halo["mg"].wait()
     stack_shifts("mg", s_mg)
 
@@ -500,8 +512,8 @@
                 stem_grad[at_, bt] = grad.astype(BF)
 
     conv(s_mg, b_mid, spans[1], half_store)
+    sums[1].step()
     sums[0].step()
-    sums[1].step()
 
     def stem_wgrad(a, b, pair):
         wgrad_into(bases[0], patch(s_feat, a, b, pair), grad_row(stem_grad, a, b, pair, 0), f0)
@@ -510,9 +522,10 @@
     sums[2].step()
     sums[0].step()
     sums[1].step()
-    for _ in range(3):
-        for item in (sums[2], sums[0], sums[1]):
-            item.step()
+    sums[2].step()
+    sums[1].step()
+    sums[2].step()
+    sums[1].step()
     for item in (sums[2], sums[0], sums[1]):
         item.finish()
     for item in halo.values():
@@ -538,6 +551,8 @@
     for c, level in [(f0, 0), (f1, 1), (f2, 2), (f1, 1), (f1, 1), (f0, 0), (f1, 1)]:
         scratch.append(pltpu.VMEM((*spans[level], c, h), F32))
     scratch.append(pltpu.VMEM((w, d, f0, h), BF))
+    for a, b in ((f0, f0), (f1, f0), (f2, f1), (f0, f1), (f1, f2)):
+        scratch.append(pltpu.VMEM((a, 27 * b), BF))
     weights = (w_stem, w_middle, w_bottom, w_rise, w_final)
     counts = [lax.axis_size(axis) for axis in Summed.order]
     unit = 16 * math.prod(counts)
@@ -564,7 +579,7 @@
             *[jax.ShapeDtypeStruct((rows, h), BF) for rows in lengths],
             jax.ShapeDtypeStruct((w // 2, d // 2, f0, h), F32),
         ),
-        in_specs=[vmem] * 11,
+        in_specs=[vmem] * 9,
         out_specs=(vmem,) * 5,
         scratch_shapes=scratch,
         compiler_params=pltpu.CompilerParams(
@@ -574,8 +589,9 @@
     )(
         features.transpose(1, 2, 0, 3),
         cotangent.transpose(1, 2, 0, 3),
-        *[forward(v) for v in weights],
-        *[backward(v) for v in weights[1:]],
+        *[v.reshape(-1, *v.shape[3:]) for v in weights[:3]],
+        *[forward(v) for v in weights[3:]],
+        *[backward(v) for v in weights[3:]],
     )
     cells = w * d * h * lax.axis_size("dep") * lax.axis_size("hgt") * lax.axis_size("wid")
     fine, mid, deep = (1.0 / math.sqrt(cells / k) for k in (1.0, 8.0, 64.0))

time: 122 us -> 117 us (0.959)
  local copies, waits for them, and re-layouts: 25.7 us -> 21 us
    reshape x5 -> x2, local copies, waits for them, and re-layouts: 6.75 us -> 2.34 us  [forward(): return v.reshape(-1, v.shape[4]).T]
    reshape x5 -> x2, local copies, waits for them, and re-layouts: 3.24 us -> 1.95 us  [backward(): v[::-1, ::-1, ::-1].reshape(27, v.shape[3], v.shape[4]).transpose(1, 0, 2)]
    unnamed x25 -> x16, local copies, waits for them, and re-layouts: 13 us -> 13 us
where the time goes in v2:
time: 117 us; the launch traced here: 116 us
  Pallas kernels  94.7 us (81%)
  local copies, waits for them, and re-layouts  21 us (18%)
    pallas_call x1, Pallas kernels, local(): pl.pallas_call(functools.partial(step_kernel, (f0, f1, f2, w, d, h)), out...  92.7 us
    unnamed x16, local copies, waits for them, and re-layouts  13 us

profile of v2, /device:TPU:0, one launch (start us, length us, event | category | flops | bytes accessed | tf_op | source)
XLA Modules:
  0.0 116.3 jit_solution(13242815184599813611)
XLA Ops:
  0.6 0.0 copy-start.4
  0.6 1.0 rev.7
  1.7 0.8 copy.29.refs_8_
  2.5 1.7 %copy_bitcast_fusion = (bf16[4,4,32,128]{3,2,1,0:T(8,128)(2,1)}, bf16[4,4,32,128]{3,2,1,0:T(8,128)(2,1)}) fusion(bf16[32,4,4,128]{3,2,1,0:T(4,128)(2,1)} %param.8, bf16[32,4,4,128]{3,2,1,0:T(4,128)(2,1)} %param.7), kind=kLoop, calls=%fused_computation | loop fusion | bytes 524288 | tf_op jit(solution)/shard_map/transpose | solution.py:591
  4.2 1.1 copy.27
  5.3 0.9 reshape.60
  6.2 0.0 copy-done.4
  6.2 0.1 rev.6
  6.3 1.1 copy.28.refs_7_
  7.4 0.8 copy.26
  8.2 1.4 %reshape.59 = bf16[5184,64]{0,1:T(8,128)(2,1)} reshape(bf16[3,3,3,192,64]{3,2,1,0,4:T(4,128)(2,1)S(1)} %copy.26) | data formatting | bytes 1327104 | tf_op jit(solution)/shard_map/reshape | solution.py:569
  9.6 92.7 %unet_step.1 = (bf16[4,4,32,128]{3,2,1,0:T(8,128)(2,1)}, bf16[2816,128]{1,0:T(8,128)(2,1)}, bf16[2560,128]{1,0:T(8,128)(2,1)}, bf16[768,128]{1,0:T(8,128)(2,1)}, f32[2,2,32,128]{3,2,1,0:T(8,128)}) custom-call(bf16[4,4,32,128]{3,2,1,0:T(8,128)(2,1)} %get-tuple-element.42.refs_0_, bf16[4,4,32,128]{3,2,1,0:T(8,128)(2,1)} %get-tuple-element.41.refs_1_, ...), custom_call_target="tpu_custom_call" | custom-call | tf_op jit(solution)/shard_map/unet_step/pallas_call | solution.py:575
  102.4 1.6 %copy.30 = bf16[32,4,4,128]{3,2,1,0:T(4,128)(2,1)} copy(bf16[32,4,4,128]{3,0,2,1:T(8,128)(2,1)} %bitcast.40) | data formatting | bytes 262144
  104.0 0.8 slice_bitcast_fusion
  104.9 0.7 copy.33
  105.5 0.0 copy-start.1
  105.5 1.1 copy-done.1
  106.7 0.0 copy-start.2
  106.7 1.1 copy-done.2
  107.7 0.0 copy-start.3
  107.7 0.9 copy-done.3
  108.7 1.9 %unpack.1 = (f32[864,32]{1,0:T(8,128)}, f32[864,64]{1,0:T(8,128)}, f32[1728,128]{1,0:T(8,128)}, f32[5184,64]{1,0:T(8,128)S(1)}, f32[2592,32]{1,0:T(8,128)S(1)}) custom-call(bf16[2816,128]{1,0:T(8,128)(2,1)S(1)} %copy-done.1, bf16[2560,128]{1,0:T(8,128)(2,1)S(1)} %copy-done.2, bf16[768,128]{1,0:T(8,128)(2,1)S(1)} %copy-done.3), custom_call_target="tpu_custom_call" | custom-call | tf_op jit(solution)/shard_map/unpack/pallas_call | solution.py:612
  110.6 0.0 copy-start
  110.6 1.1 copy-done
  111.7 2.5 %copy.32 = f32[3,3,3,96,32]{3,4,2,1,0:T(8,128)} copy(f32[3,3,3,96,32]{4,3,2,1,0:T(8,128)} %bitcast.32) | data formatting | bytes 663552
  114.1 2.2 %copy.31 = f32[3,3,3,192,64]{3,4,2,1,0:T(8,128)} copy(f32[3,3,3,192,64]{4,3,2,1,0:T(8,128)S(1)} %bitcast.31) | data formatting | bytes 2654208
Async XLA Ops:
  0.6 5.6 %copy-start.4 = (bf16[3,3,3,192,64]{3,4,2,1,0:T(8,128)(2,1)S(1)}, bf16[3,3,3,192,64]{3,4,2,1,0:T(8,128)(2,1)}, u32[]{:S(2)}) copy-start(bf16[3,3,3,192,64]{3,4,2,1,0:T(8,128)(2,1)} %param.12) | copy-start | bytes 1990660
  105.5 1.1 copy-start.1
  106.7 1.1 copy-start.2
  107.7 0.9 copy-start.3
  110.6 1.1 copy-start

commit v3 on v2

--- a/solution.py
+++ b/solution.py
@@ -320,7 +320,7 @@
         return parts[0] if pair == 1 else jnp.concatenate(parts, axis=1)
 
     def over_rows(span, body):
-        pair = 2 if span[1] % 2 == 0 else 1
+        pair = 4 if span[1] % 4 == 0 else 2 if span[1] % 2 == 0 else 1
         across = span[1] // pair
 
         def trip(i, _):
@@ -344,13 +344,15 @@
     def wgrad_into(base, patches, grad, width):
         groups = lanes // width
         count = patches.shape[0] // groups
+        value = None
         for g in range(groups):
             pieces = [jnp.zeros_like(grad)] * groups
             pieces[g] = grad
             full = pieces[0] if groups == 1 else jnp.concatenate(pieces, axis=0)
-            value = mm_nt(patches[g * count : (g + 1) * count], full)
-            where = sums[base[0]].total
-            where[base[1] : base[1] + count] += value
+            piece = mm_nt(patches[g * count : (g + 1) * count], full)
+            value = piece if value is None else value + piece
+        where = sums[base[0]].total
+        where[base[1] : base[1] + count] += value
 
     def grad_row(ref, a, b, pair, pad):
         parts = [ref[a + pad, b + pad + q] for q in range(pair)]

time: 117 us -> 116 us (level)
  no operation moved by 1% of the time
where the time goes in v3:
time: 116 us
  Pallas kernels  94.1 us (81%)
  local copies, waits for them, and re-layouts  21 us (18%)
    pallas_call x1, Pallas kernels, local(): pl.pallas_call(functools.partial(step_kernel, (f0, f1, f2, w, d, h)), out...  92.2 us
    unnamed x16, local copies, waits for them, and re-layouts  13 us
    reshape x2, local copies, waits for them, and re-layouts, forward(): return v.reshape(-1, v.shape[4]).T  2.34 us

profile of v3, /device:TPU:0, one launch (start us, length us, event | category | flops | bytes accessed | tf_op | source)
XLA Modules:
  0.0 115.8 jit_solution(14220912346380979280)
XLA Ops:
  0.6 0.0 copy-start.4
  0.6 1.0 rev.7
  1.7 0.8 copy.29.refs_8_
  2.5 1.7 %copy_bitcast_fusion = (bf16[4,4,32,128]{3,2,1,0:T(8,128)(2,1)}, bf16[4,4,32,128]{3,2,1,0:T(8,128)(2,1)}) fusion(bf16[32,4,4,128]{3,2,1,0:T(4,128)(2,1)} %param.8, bf16[32,4,4,128]{3,2,1,0:T(4,128)(2,1)} %param.7), kind=kLoop, calls=%fused_computation | loop fusion | bytes 524288 | tf_op jit(solution)/shard_map/transpose | solution.py:593
  4.2 1.1 copy.27
  5.3 0.9 reshape.60
  6.2 0.0 copy-done.4
  6.2 0.1 rev.6
  6.3 1.1 copy.28.refs_7_
  7.4 0.8 copy.26
  8.2 1.4 %reshape.59 = bf16[5184,64]{0,1:T(8,128)(2,1)} reshape(bf16[3,3,3,192,64]{3,2,1,0,4:T(4,128)(2,1)S(1)} %copy.26) | data formatting | bytes 1327104 | tf_op jit(solution)/shard_map/reshape | solution.py:571
  9.6 92.2 %unet_step.1 = (bf16[4,4,32,128]{3,2,1,0:T(8,128)(2,1)}, bf16[2816,128]{1,0:T(8,128)(2,1)}, bf16[2560,128]{1,0:T(8,128)(2,1)}, bf16[768,128]{1,0:T(8,128)(2,1)}, f32[2,2,32,128]{3,2,1,0:T(8,128)}) custom-call(bf16[4,4,32,128]{3,2,1,0:T(8,128)(2,1)} %get-tuple-element.42.refs_0_, bf16[4,4,32,128]{3,2,1,0:T(8,128)(2,1)} %get-tuple-element.41.refs_1_, ...), custom_call_target="tpu_custom_call" | custom-call | tf_op jit(solution)/shard_map/unet_step/pallas_call | solution.py:577
  101.8 1.6 %copy.30 = bf16[32,4,4,128]{3,2,1,0:T(4,128)(2,1)} copy(bf16[32,4,4,128]{3,0,2,1:T(8,128)(2,1)} %bitcast.40) | data formatting | bytes 262144
  103.4 0.8 slice_bitcast_fusion
  104.3 0.7 copy.33
  105.0 0.0 copy-start.1
  105.0 1.1 copy-done.1
  106.1 0.0 copy-start.2
  106.1 1.1 copy-done.2
  107.2 0.0 copy-start.3
  107.2 0.9 copy-done.3
  108.1 1.9 %unpack.1 = (f32[864,32]{1,0:T(8,128)}, f32[864,64]{1,0:T(8,128)}, f32[1728,128]{1,0:T(8,128)}, f32[5184,64]{1,0:T(8,128)S(1)}, f32[2592,32]{1,0:T(8,128)S(1)}) custom-call(bf16[2816,128]{1,0:T(8,128)(2,1)S(1)} %copy-done.1, bf16[2560,128]{1,0:T(8,128)(2,1)S(1)} %copy-done.2, bf16[768,128]{1,0:T(8,128)(2,1)S(1)} %copy-done.3), custom_call_target="tpu_custom_call" | custom-call | tf_op jit(solution)/shard_map/unpack/pallas_call | solution.py:614
  110.0 0.0 copy-start
  110.0 1.1 copy-done
  111.1 2.5 %copy.32 = f32[3,3,3,96,32]{3,4,2,1,0:T(8,128)} copy(f32[3,3,3,96,32]{4,3,2,1,0:T(8,128)} %bitcast.32) | data formatting | bytes 663552
  113.6 2.2 %copy.31 = f32[3,3,3,192,64]{3,4,2,1,0:T(8,128)} copy(f32[3,3,3,192,64]{4,3,2,1,0:T(8,128)S(1)} %bitcast.31) | data formatting | bytes 2654208
Async XLA Ops:
  0.6 5.6 %copy-start.4 = (bf16[3,3,3,192,64]{3,4,2,1,0:T(8,128)(2,1)S(1)}, bf16[3,3,3,192,64]{3,4,2,1,0:T(8,128)(2,1)}, u32[]{:S(2)}) copy-start(bf16[3,3,3,192,64]{3,4,2,1,0:T(8,128)(2,1)} %param.12) | copy-start | bytes 1990660
  105.0 1.1 copy-start.1
  106.1 1.1 copy-start.2
  107.2 0.9 copy-start.3
  110.0 1.1 copy-start
